TPU v7x, 32 devices: a whole 2x2x4 slice. The times are simulated.
32 devices in a mesh: grp: 2 (over y), row: 8 (over z, x), col: 2 (over core).
Axes of the slice: x: 2, y: 2, z: 4, core: 2. Of those that a mesh axis runs over, the one named last changes fastest.
Arguments:
- grad_out: bfloat16 [1024, 8192], P(('grp', 'row'), 'col'), parts along dimension 0, may hold values from -6 to 6
- hidden_act: bfloat16 [1024, 22016], P(('grp', 'col'), 'row'), parts along dimension 0, may hold values from -6 to 6
- down_weight: bfloat16 [22016, 8192], P('row', 'col'), may hold values from -0.0390625 to 0.0390625
- proj_in: bfloat16 [22016, 64], P('row'), may hold values from -0.0390625 to 0.0390625
- proj_out: bfloat16 [8192, 64], P('col'), may hold values from -0.0625 to 0.0625
- queries: bfloat16 [128, 4096], P('row', 'col'), may hold values from -0.01171875 to 0.01171875
- example_ids: int32 [1024], P(('grp', 'row')), parts along dimension 0, may hold values from 0 to 7, never falling along the last dimension, each value on 1 to 128 neighbouring positions
Outputs:
- grad_hidden: bfloat16 [1024, 22016], P(('grp', 'col'), 'row'), parts along dimension 0
- weight_grad: bfloat16 [44032, 8192], P(('grp', 'row'), 'col'), parts along dimension 0
- scores: float32 [128, 16], P(('row', 'col'), 'grp'), parts along dimension 1
There are 2 independent parts, one for each index of `grp`. A program takes and returns all parts, laid end to end along the dimension named above; an argument that names none is the same for every part. Nothing has to cross between parts.
Inputs may be any that keep to these rules, and one draw needn't show every extreme that they name: `example_ids`: never falling along the tokens; each example holds 1 to 128 tokens, one exactly 128.
All inputs are finite; a program needn't handle non-finite values.
Results may differ from a plain program's by a relative error of at most 0.001.
Values may be sent and summed in bfloat16 or wider, within the bound.
A program may use at most 192 MiB of HBM per device.

v0:
```python
import jax
import jax.numpy as jnp
from jax import lax
from jax.sharding import PartitionSpec as P

EXAMPLES = 8


def body(grad_out, hidden_act, down_weight, proj_in, proj_out, queries, example_ids):
    full_hidden = lax.all_gather(hidden_act, "col", axis=0, tiled=True)
    full_grad = lax.all_gather(grad_out, "row", axis=0, tiled=True)
    token_rows = full_grad
    grad_hidden = lax.psum_scatter(
        lax.dot_general(
            token_rows, down_weight, (((1,), (1,)), ((), ())), preferred_element_type=jnp.float32
        ),
        "col",
        scatter_dimension=0,
        tiled=True,
    ).astype(jnp.bfloat16)
    weight_grad = lax.dot_general(
        full_hidden, full_grad, (((0,), (0,)), ((), ())), preferred_element_type=jnp.float32
    ).astype(jnp.bfloat16)
    token_rows = full_hidden
    in_factor = lax.psum_scatter(
        jnp.dot(token_rows, proj_in, preferred_element_type=jnp.float32),
        "row",
        scatter_dimension=0,
        tiled=True,
    )
    out_factor = lax.psum(jnp.dot(grad_out, proj_out, preferred_element_type=jnp.float32), "col")
    split_rank = in_factor.shape[1] // lax.axis_size("col")
    own_factor = lax.dynamic_slice_in_dim(
        in_factor, lax.axis_index("col") * split_rank, split_rank, 1
    )
    outer_terms = (own_factor[:, :, None] * out_factor[:, None, :]).reshape(own_factor.shape[0], -1)
    labels = jnp.arange(EXAMPLES, dtype=jnp.int32)
    onehot = (example_ids[None, :] == labels[:, None]).astype(jnp.float32)
    partial_grads = jnp.dot(onehot, outer_terms, precision=lax.Precision.HIGHEST)
    example_grads = lax.psum(partial_grads, "row")
    values = jnp.dot(queries.astype(jnp.float32), example_grads.T, precision=lax.Precision.HIGHEST)
    scores = lax.psum_scatter(values, "col", scatter_dimension=0, tiled=True)
    return (grad_hidden, weight_grad, scores)


def solution(mesh):
    return jax.shard_map(
        body,
        mesh=mesh,
        in_specs=(
            P(("grp", "row"), "col"),
            P(("grp", "col"), "row"),
            P("row", "col"),
            P("row", None),
            P("col", None),
            P("row", "col"),
            P(("grp", "row")),
        ),
        out_specs=(P(("grp", "col"), "row"), P(("grp", "row"), "col"), P(("row", "col"), "grp")),
        check_vma=False,
    )
```

profile of v0, /device:TPU:0, one launch (start us, length us, event | category | flops | bytes accessed | tf_op | source)
XLA Modules:
  0.0 267.6 jit_solution(11298728215527538428)
XLA Ops:
  7.2 0.7 all-gather.5.cloned.1.call-update
  8.0 15.3 %all-gather.5.cloned.1.call-done = bf16[512,2752]{0,1:T(8,128)(2,1)} async-done(((bf16[256,2752]{0,1:T(8,128)(2,1)}), bf16[512,2752]{0,1:T(8,128)(2,1)}) %all-gather.5.cloned.1.call-update) | async-done | bytes 2818064 | tf_op jit(solution)/shard_map/all_gather | solution.py:10
  23.3 3.5 %fusion.3 = f32[512,64]{1,0:T(8,128)} fusion(bf16[512,2752]{0,1:T(8,128)(2,1)} %all-gather.5.cloned.1.call-done, bf16[2752,64]{0,1:T(8,128)(2,1)} %param.10), kind=kOutput, calls=%fused_computation.9 | convolution fusion | flops 180355072 | bytes 3301376 | tf_op jit(solution)/shard_map/dot_general | solution.py:26
  26.8 0.0 all-gather.3.cloned.1.call-start
  26.9 0.7 all-gather.3.cloned.1.call-update
  27.6 0.3 fusion.4
  27.9 3.5 %psum.14 = f32[64,64]{1,0:T(8,128)S(1)} all-reduce(f32[64,64]{1,0:T(8,128)S(1)} %fusion.4), channel_id=1, replica_groups=mesh['grp'=2,'row'=8,'col'=2] {'col'}, use_global_device_ids=true, to_apply=%region_2.0 | all-reduce | flops 4096 | bytes 32768 | tf_op jit(solution)/shard_map/psum | solution.py:31
  31.4 59.1 %reduce-scatter.6.cloned.1.call-done = f32[64,64]{1,0:T(8,128)} async-done(((f32[512,64]{1,0:T(8,128)}), f32[64,64]{1,0:T(8,128)}) %reduce-scatter.6.cloned.1.call-update) | async-done | bytes 16400 | tf_op jit(solution)/shard_map/reduce_scatter | solution.py:25
  90.5 0.8 constant_dynamic-slice_fusion.1
  91.3 0.3 broadcast_multiply_fusion
  91.7 0.4 mul.24
  92.1 0.9 fusion
  93.0 0.0 reduce-scatter.4.cloned.1.call-start
  93.1 71.5 %all-gather.3.cloned.1.call-done = bf16[512,4096]{1,0:T(8,128)(2,1)} async-done(((bf16[64,4096]{1,0:T(8,128)(2,1)}), bf16[512,4096]{1,0:T(8,128)(2,1)}) %all-gather.3.cloned.1.call-update) | async-done | bytes 4194320 | tf_op jit(solution)/shard_map/all_gather | solution.py:11
  164.5 19.1 %fusion.2 = f32[512,2752]{0,1:T(8,128)} fusion(bf16[512,4096]{1,0:T(8,128)(2,1)} %all-gather.3.cloned.1.call-done, bf16[2752,4096]{1,0:T(8,128)(2,1)} %param.9), kind=kOutput, calls=%fused_computation.8 | convolution fusion | flops 11542724608 | bytes 32374784 | tf_op jit(solution)/shard_map/dot_general | solution.py:14
  183.7 0.6 copy-done.5
  184.3 0.6 dynamic-slice
  185.5 50.7 %all-reduce.3.cloned.1.call-done = f32[8,2048]{1,0:T(8,128)} async-done(((f32[8,2048]{1,0:T(8,128)}), f32[8,2048]{1,0:T(8,128)}) %all-reduce.3.cloned.1.call-update) | async-done | bytes 65552 | tf_op jit(solution)/shard_map/psum | solution.py:40
  236.2 1.0 convolution_bitcast_fusion
  237.2 2.5 all-reduce
  239.7 0.1 constant_dynamic-slice_fusion
  239.8 0.7 copy.11
  240.5 17.6 %convolution_convert_fusion = bf16[2752,4096]{1,0:T(8,128)(2,1)} fusion(bf16[512,2752]{0,1:T(8,128)(2,1)S(1)} %copy-done.4, bf16[512,4096]{1,0:T(8,128)(2,1)} %all-gather.3.cloned.1.call-done), kind=kOutput, calls=%fused_computation | convolution fusion | flops 11553996800 | bytes 29556736 | tf_op jit(solution)/shard_map/dot_general | solution.py:21
  258.0 3.0 %convert_element_type.8 = bf16[256,2752]{0,1:T(8,128)(2,1)} convert(f32[256,2752]{0,1:T(8,128)} %reduce-scatter.4.cloned.1.call-done) | non-fusion elementwise | flops 704512 | bytes 4227072 | tf_op jit(solution)/shard_map/convert_element_type | solution.py:20
  (18 shorter events, 0.2 us)
Async XLA Ops:
  7.2 20.5 %copy-start = (bf16[4096,64]{0,1:T(8,128)(2,1)S(1)}, bf16[4096,64]{0,1:T(8,128)(2,1)}, u32[]{:S(2)}) copy-start(bf16[4096,64]{0,1:T(8,128)(2,1)} %param.11) | copy-start | bytes 1572868
  7.2 20.4 %copy-start.1 = (bf16[64,4096]{1,0:T(8,128)(2,1)S(1)}, bf16[64,4096]{1,0:T(8,128)(2,1)}, u32[]{:S(2)}) copy-start(bf16[64,4096]{1,0:T(8,128)(2,1)} %param.7) | copy-start | bytes 1572868
  7.2 16.1 %all-gather.5.cloned.1.call-start = ((), (), s32[]{:S(2)}) async-start(), calls=%async_computation.4 | async-start | bytes 4227072 | tf_op jit(solution)/shard_map/all_gather | solution.py:10
  7.9 84.1 %copy-start.3 = (s32[64]{0:T(128)S(1)}, s32[64]{0:T(128)}, u32[]{:S(2)}) copy-start(s32[64]{0:T(128)} %param.13) | copy-start | bytes 772
  7.9 82.6 %reduce-scatter.6.cloned.1.call-start = ((), (), s32[]{:S(2)}) async-start(), calls=%async_computation.5 | async-start | bytes 294912 | tf_op jit(solution)/shard_map/reduce_scatter | solution.py:25
  26.8 137.7 %all-gather.3.cloned.1.call-start = ((), (), s32[]{:S(2)}) async-start(), calls=%async_computation.2 | async-start | bytes 4718592 | tf_op jit(solution)/shard_map/all_gather | solution.py:11
  27.6 208.7 %all-reduce.3.cloned.1.call-start = ((), (), s32[]{:S(2)}) async-start(), calls=%async_computation.6 | async-start | bytes 131072 | tf_op jit(solution)/shard_map/psum | solution.py:40
  93.0 165.0 %reduce-scatter.4.cloned.1.call-start = ((), (), s32[]{:S(2)}) async-start(), calls=%async_computation.3 | async-start | bytes 8454144 | tf_op jit(solution)/shard_map/reduce_scatter | solution.py:13
  183.6 0.7 copy-start.5
  183.6 52.6 %copy-start.2 = (bf16[16,2048]{1,0:T(8,128)(2,1)S(1)}, bf16[16,2048]{1,0:T(8,128)(2,1)}, u32[]{:S(2)}) copy-start(bf16[16,2048]{1,0:T(8,128)(2,1)} %param.12) | copy-start | bytes 196612
  183.6 56.8 %copy-start.4 = (bf16[512,2752]{0,1:T(8,128)(2,1)S(1)}, bf16[512,2752]{0,1:T(8,128)(2,1)}, u32[]{:S(2)}) copy-start(bf16[512,2752]{0,1:T(8,128)(2,1)} %all-gather.5.cloned.1.call-done) | copy-start | bytes 8454148
Sparse Core Ops, SparseCore 0:
  9.5 13.7 all-gather.4
  27.2 63.2 reduce-scatter.5
  92.6 71.8 all-gather.2
  168.4 67.8 all-reduce.2
  238.4 13.1 reduce-scatter.3
where the time goes:
time: 268 us
  waiting for transfers between devices  198 us (74%)
  matrix products  42.3 us (16%)
  between operations  14.5 us (5%)
  blocking collectives  5.99 us (2%)
  other arithmetic  3.36 us (1%)
  local copies, waits for them, and re-layouts  3.16 us (1%)
    all_gather x1, waiting for transfers between devices, body(): full_grad = lax.all_gather(grad_out, 'row', axis=0, tiled=True)  71.5 us
    reduce_scatter x1, waiting for transfers between devices, body(): lax.psum_scatter(jnp.dot(token_rows, proj_in, preferred_element_type=jnp....  59.1 us
    psum x1, waiting for transfers between devices, body(): example_grads = lax.psum(partial_grads, 'row')  50.7 us
    dot_general x1, matrix products, body(): lax.dot_general(token_rows, down_weight, (((1,), (1,)), ((), ())), prefer...  19.1 us
    dot_general x1, matrix products, body(): lax.dot_general(full_hidden, full_grad, (((0,), (0,)), ((), ())), preferr...  17.6 us
    all_gather x1, waiting for transfers between devices, body(): full_hidden = lax.all_gather(hidden_act, 'col', axis=0, tiled=True)  15.3 us
  transfers between devices with their start and end apart: 5, of which 4 were waited for; matrix products, arithmetic and copies ran while one was open for 16% of the time, Pallas kernels for 0%

commit v1 on v0

--- a/solution.py
+++ b/solution.py
@@ -8,7 +8,12 @@
 
 def body(grad_out, hidden_act, down_weight, proj_in, proj_out, queries, example_ids):
     full_hidden = lax.all_gather(hidden_act, "col", axis=0, tiled=True)
-    full_grad = lax.all_gather(grad_out, "row", axis=0, tiled=True)
+    ring = [grad_out]
+    for hop in range(7):
+        ring.append(lax.ppermute(ring[-1], "row", [(dev, (dev + 1) % 8) for dev in range(8)]))
+    full_grad = jnp.roll(
+        jnp.concatenate(ring[::-1], axis=0), (lax.axis_index("row") + 1) * ring[0].shape[0], axis=0
+    )
     token_rows = full_grad
     grad_hidden = lax.psum_scatter(
         lax.dot_general(

time: 268 us -> 258 us (0.963)
  waiting for transfers between devices: 198 us -> 171 us
  local copies, waits for them, and re-layouts: 3.16 us -> 14.5 us
  starting transfers between devices: 0.2 us -> 3.19 us
    ppermute x0 -> x7, waiting for transfers between devices: none -> 77.1 us  [body(): lax.ppermute(ring[-1], 'row', [(dev, (dev + 1) % 8) for dev in range(8)])]
    all_gather x1 -> x0, waiting for transfers between devices: 71.5 us -> none  [body(): full_grad = lax.all_gather(grad_out, 'row', axis=0, tiled=True)]
    all_gather x1, waiting for transfers between devices: 15.3 us -> 0.01 us  [body(): full_hidden = lax.all_gather(hidden_act, 'col', axis=0, tiled=True)]
    psum x1, waiting for transfers between devices: 50.7 us -> 38.7 us  [body(): example_grads = lax.psum(partial_grads, 'row')]
    unnamed x15 -> x44, local copies, waits for them, and re-layouts: 1.97 us -> 13.3 us
    reduce_scatter x1, waiting for transfers between devices: 59.1 us -> 55 us  [body(): lax.psum_scatter(jnp.dot(token_rows, proj_in, preferred_element_type=jnp....]
    ppermute x0 -> x7, starting transfers between devices: none -> 3.04 us  [body(): lax.ppermute(ring[-1], 'row', [(dev, (dev + 1) % 8) for dev in range(8)])]
  transfers between devices with their start and end apart: 5 -> 11, of which waited for: 4 -> 8; matrix products, arithmetic and copies ran while one was open for 16% -> 21% of each run, Pallas kernels for 0% -> 0%
where the time goes in v1:
time: 258 us; the launch traced here: 257 us
  waiting for transfers between devices  171 us (66%)
  matrix products  43.8 us (17%)
  between operations  14.7 us (6%)
  local copies, waits for them, and re-layouts  14.5 us (6%)
  blocking collectives  5.91 us (2%)
  other arithmetic  3.36 us (1%)
  starting transfers between devices  3.19 us (1%)
    ppermute x7, waiting for transfers between devices, body(): lax.ppermute(ring[-1], 'row', [(dev, (dev + 1) % 8) for dev in range(8)])  77.1 us
    reduce_scatter x1, waiting for transfers between devices, body(): lax.psum_scatter(jnp.dot(token_rows, proj_in, preferred_element_type=jnp....  55 us
    psum x1, waiting for transfers between devices, body(): example_grads = lax.psum(partial_grads, 'row')  38.7 us
    dot_general x1, matrix products, body(): lax.dot_general(full_hidden, full_grad, (((0,), (0,)), ((), ())), preferr...  18.9 us
    dot_general x1, matrix products, body(): lax.dot_general(token_rows, down_weight, (((1,), (1,)), ((), ())), prefer...  18 us
    unnamed x44, local copies, waits for them, and re-layouts  13.3 us
  transfers between devices with their start and end apart: 11, of which 8 were waited for; matrix products, arithmetic and copies ran while one was open for 21% of the time, Pallas kernels for 0%

profile of v1, /device:TPU:0, one launch (start us, length us, event | category | flops | bytes accessed | tf_op | source)
XLA Modules:
  0.0 256.9 jit_solution(655318566692774925)
XLA Ops:
  8.0 3.0 %collective-permute-start = (bf16[64,4096]{1,0:T(8,128)(2,1)}, bf16[64,4096]{1,0:T(8,128)(2,1)S(1)}, u32[]{:S(2)}, u32[]{:S(2)}) collective-permute-start(bf16[64,4096]{1,0:T(8,128)(2,1)} %param.7), channel_id=1, source_target_pairs={{0,2},{2,4},{4,6},{6,8},{8,10},{10,12},{12,14},{14,0},{1,3},{3,5},... | collective-permute-start | bytes 1572872 | tf_op jit(solution)/shard_map/ppermute | solution.py:13
  11.0 15.2 %collective-permute-done = bf16[64,4096]{1,0:T(8,128)(2,1)S(1)} collective-permute-done((bf16[64,4096]{1,0:T(8,128)(2,1)}, bf16[64,4096]{1,0:T(8,128)(2,1)S(1)}, u32[]{:S(2)}, u32[]{:S(2)}) %collective-permute-start) | collective-permute-done | bytes 524320 | tf_op jit(solution)/shard_map/ppermute | solution.py:13
  26.2 15.8 %collective-permute-done.1 = bf16[64,4096]{1,0:T(8,128)(2,1)S(1)} collective-permute-done((bf16[64,4096]{1,0:T(8,128)(2,1)S(1)}, bf16[64,4096]{1,0:T(8,128)(2,1)S(1)}, u32[]{:S(2)}, u32[]{:S(2)}) %collective-permute-start.1) | collective-permute-done | bytes 524320 | tf_op jit(solution)/shard_map/ppermute | solution.py:13
  42.0 14.9 %collective-permute-done.2 = bf16[64,4096]{1,0:T(8,128)(2,1)S(1)} collective-permute-done((bf16[64,4096]{1,0:T(8,128)(2,1)S(1)}, bf16[64,4096]{1,0:T(8,128)(2,1)S(1)}, u32[]{:S(2)}, u32[]{:S(2)}) %collective-permute-start.2) | collective-permute-done | bytes 524320 | tf_op jit(solution)/shard_map/ppermute | solution.py:13
  57.7 14.1 %collective-permute-done.3 = bf16[64,4096]{1,0:T(8,128)(2,1)S(1)} collective-permute-done((bf16[64,4096]{1,0:T(8,128)(2,1)S(1)}, bf16[64,4096]{1,0:T(8,128)(2,1)S(1)}, u32[]{:S(2)}, u32[]{:S(2)}) %collective-permute-start.3) | collective-permute-done | bytes 524320 | tf_op jit(solution)/shard_map/ppermute | solution.py:13
  71.8 13.2 %collective-permute-done.4 = bf16[64,4096]{1,0:T(8,128)(2,1)S(1)} collective-permute-done((bf16[64,4096]{1,0:T(8,128)(2,1)S(1)}, bf16[64,4096]{1,0:T(8,128)(2,1)S(1)}, u32[]{:S(2)}, u32[]{:S(2)}) %collective-permute-start.4) | collective-permute-done | bytes 524320 | tf_op jit(solution)/shard_map/ppermute | solution.py:13
  85.0 3.7 %fusion.8 = f32[512,64]{1,0:T(8,128)} fusion(bf16[512,2752]{0,1:T(8,128)(2,1)} %all-gather.2.cloned.1.call-done, bf16[2752,64]{0,1:T(8,128)(2,1)} %param.10), kind=kOutput, calls=%fused_computation.30 | convolution fusion | flops 180355072 | bytes 3301376 | tf_op jit(solution)/shard_map/dot_general | solution.py:31
  88.7 1.3 fusion.9
  90.1 3.4 %psum.14 = f32[64,64]{1,0:T(8,128)S(1)} all-reduce(f32[64,64]{1,0:T(8,128)S(1)} %fusion.9), channel_id=1, replica_groups=mesh['grp'=2,'row'=8,'col'=2] {'col'}, use_global_device_ids=true, to_apply=%region_2.3 | all-reduce | flops 4096 | bytes 32768 | tf_op jit(solution)/shard_map/psum | solution.py:36
  93.5 4.0 %collective-permute-done.5 = bf16[64,4096]{1,0:T(8,128)(2,1)} collective-permute-done((bf16[64,4096]{1,0:T(8,128)(2,1)S(1)}, bf16[64,4096]{1,0:T(8,128)(2,1)}, u32[]{:S(2)}, u32[]{:S(2)}) %collective-permute-start.5) | collective-permute-done | bytes 524320 | tf_op jit(solution)/shard_map/ppermute | solution.py:13
  97.5 55.0 %reduce-scatter.6.cloned.1.call-done = f32[64,64]{1,0:T(8,128)} async-done(((f32[512,64]{1,0:T(8,128)}), f32[64,64]{1,0:T(8,128)}) %reduce-scatter.6.cloned.1.call-update) | async-done | bytes 16400 | tf_op jit(solution)/shard_map/reduce_scatter | solution.py:30
  155.0 1.1 constant_dynamic-update-slice_fusion.15
  156.1 1.1 constant_dynamic-update-slice_fusion.14
  157.2 1.1 constant_dynamic-update-slice_fusion.13
  158.3 1.1 constant_dynamic-update-slice_fusion.12
  159.4 1.1 constant_dynamic-update-slice_fusion.11
  160.6 1.1 constant_dynamic-update-slice_fusion.7
  161.7 1.1 constant_dynamic-update-slice_fusion.6
  163.1 3.2 %copy-done.10 = bf16[1024,4096]{1,0:T(8,128)(2,1)} copy-done((bf16[1024,4096]{1,0:T(8,128)(2,1)}, bf16[1024,4096]{1,0:T(8,128)(2,1)S(1)}, u32[]{:S(2)}) %copy-start.10) | copy-done | bytes 8388632
  166.3 18.0 %fusion.2 = f32[512,2752]{0,1:T(8,128)} fusion(bf16[2752,4096]{1,0:T(8,128)(2,1)} %param.9, bf16[1024,4096]{1,0:T(8,128)(2,1)S(1)} %constant_dynamic-update-slice_fusion, s32[]{:T(128)S(6)} %select_n.17), kind=kOutput, calls=%fused_computation.3 | convolution fusion | flops 11542724608 | bytes 32374788 | tf_op jit(solution)/shard_map/dot_general | solution.py:19
  185.6 38.7 %all-reduce.3.cloned.1.call-done = f32[8,2048]{1,0:T(8,128)} async-done(((f32[8,2048]{1,0:T(8,128)}), f32[8,2048]{1,0:T(8,128)}) %all-reduce.3.cloned.1.call-update) | async-done | bytes 65552 | tf_op jit(solution)/shard_map/psum | solution.py:45
  225.2 2.5 all-reduce
  228.4 18.9 %fusion = bf16[2752,4096]{1,0:T(8,128)(2,1)} fusion(bf16[512,2752]{0,1:T(8,128)(2,1)} %all-gather.2.cloned.1.call-done, bf16[1024,4096]{1,0:T(8,128)(2,1)} %copy-done.10, s32[]{:T(128)S(6)} %select_n.17), kind=kOutput, calls=%fused_computation.1 | convolution fusion | flops 11553996800 | bytes 29556740 | tf_op jit(solution)/shard_map/dot_general | solution.py:26
  247.3 3.0 %convert_element_type.11 = bf16[256,2752]{0,1:T(8,128)(2,1)} convert(f32[256,2752]{0,1:T(8,128)} %reduce-scatter.4.cloned.1.call-done) | non-fusion elementwise | flops 704512 | bytes 4227072 | tf_op jit(solution)/shard_map/convert_element_type | solution.py:25
  (59 shorter events, 6.8 us)
Async XLA Ops:
  7.2 81.6 %copy-start = (bf16[4096,64]{0,1:T(8,128)(2,1)S(1)}, bf16[4096,64]{0,1:T(8,128)(2,1)}, u32[]{:S(2)}) copy-start(bf16[4096,64]{0,1:T(8,128)(2,1)} %param.11) | copy-start | bytes 1572868
  7.2 153.4 %copy-start.2 = (bf16[64,4096]{1,0:T(8,128)(2,1)S(1)}, bf16[64,4096]{1,0:T(8,128)(2,1)}, u32[]{:S(2)}) copy-start(bf16[64,4096]{1,0:T(8,128)(2,1)} %param.7) | copy-start | bytes 1572868
  7.2 146.8 %copy-start.11 = (s32[64]{0:T(128)S(1)}, s32[64]{0:T(128)}, u32[]{:S(2)}) copy-start(s32[64]{0:T(128)} %param.13) | copy-start | bytes 772
  7.2 77.8 %all-gather.2.cloned.1.call-start = ((), (), s32[]{:S(2)}) async-start(), calls=%async_computation.3 | async-start | bytes 4227072 | tf_op jit(solution)/shard_map/all_gather | solution.py:10
  7.9 144.5 %reduce-scatter.6.cloned.1.call-start = ((), (), s32[]{:S(2)}) async-start(), calls=%async_computation.4 | async-start | bytes 294912 | tf_op jit(solution)/shard_map/reduce_scatter | solution.py:30
  8.0 18.2 %collective-permute-start = (bf16[64,4096]{1,0:T(8,128)(2,1)}, bf16[64,4096]{1,0:T(8,128)(2,1)S(1)}, u32[]{:S(2)}, u32[]{:S(2)}) collective-permute-start(bf16[64,4096]{1,0:T(8,128)(2,1)} %param.7), channel_id=1, source_target_pairs={{0,2},{2,4},{4,6},{6,8},{8,10},{10,12},{12,14},{14,0},{1,3},{3,5},... | collective-permute-start | bytes 1572872 | tf_op jit(solution)/shard_map/ppermute | solution.py:13
  26.2 15.8 %collective-permute-start.1 = (bf16[64,4096]{1,0:T(8,128)(2,1)S(1)}, bf16[64,4096]{1,0:T(8,128)(2,1)S(1)}, u32[]{:S(2)}, u32[]{:S(2)}) collective-permute-start(bf16[64,4096]{1,0:T(8,128)(2,1)S(1)} %collective-permute-done), channel_id=1, source_target_pairs={{0,2},{2,4},{4,6},{6,8},{8,10},{10,12},{12,14},{14,0},{1,3},{3,5},... | collective-permute-start | bytes 1572872 | tf_op jit(solution)/shard_map/ppermute | solution.py:13
  42.0 14.9 %collective-permute-start.2 = (bf16[64,4096]{1,0:T(8,128)(2,1)S(1)}, bf16[64,4096]{1,0:T(8,128)(2,1)S(1)}, u32[]{:S(2)}, u32[]{:S(2)}) collective-permute-start(bf16[64,4096]{1,0:T(8,128)(2,1)S(1)} %collective-permute-done.1), channel_id=1, source_target_pairs={{0,2},{2,4},{4,6},{6,8},{8,10},{10,12},{12,14},{14,0},{1,3},{3,5},... | collective-permute-start | bytes 1572872 | tf_op jit(solution)/shard_map/ppermute | solution.py:13
  56.9 0.8 copy-start.3
  57.7 14.1 %collective-permute-start.3 = (bf16[64,4096]{1,0:T(8,128)(2,1)S(1)}, bf16[64,4096]{1,0:T(8,128)(2,1)S(1)}, u32[]{:S(2)}, u32[]{:S(2)}) collective-permute-start(bf16[64,4096]{1,0:T(8,128)(2,1)S(1)} %collective-permute-done.2), channel_id=1, source_target_pairs={{0,2},{2,4},{4,6},{6,8},{8,10},{10,12},{12,14},{14,0},{1,3},{3,5},... | collective-permute-start | bytes 1572872 | tf_op jit(solution)/shard_map/ppermute | solution.py:13
  71.8 80.7 %copy-start.5 = (bf16[64,4096]{1,0:T(8,128)(2,1)}, bf16[64,4096]{1,0:T(8,128)(2,1)S(1)}, u32[]{:S(2)}) copy-start(bf16[64,4096]{1,0:T(8,128)(2,1)S(1)} %collective-permute-done.3) | copy-start | bytes 1572868
  71.8 13.2 %collective-permute-start.4 = (bf16[64,4096]{1,0:T(8,128)(2,1)S(1)}, bf16[64,4096]{1,0:T(8,128)(2,1)S(1)}, u32[]{:S(2)}, u32[]{:S(2)}) collective-permute-start(bf16[64,4096]{1,0:T(8,128)(2,1)S(1)} %collective-permute-done.3), channel_id=1, source_target_pairs={{0,2},{2,4},{4,6},{6,8},{8,10},{10,12},{12,14},{14,0},{1,3},{3,5},... | collective-permute-start | bytes 1572872 | tf_op jit(solution)/shard_map/ppermute | solution.py:13
  85.0 67.4 %copy-start.7 = (bf16[64,4096]{1,0:T(8,128)(2,1)}, bf16[64,4096]{1,0:T(8,128)(2,1)S(1)}, u32[]{:S(2)}) copy-start(bf16[64,4096]{1,0:T(8,128)(2,1)S(1)} %collective-permute-done.4) | copy-start | bytes 1572868
  85.0 12.5 %collective-permute-start.5 = (bf16[64,4096]{1,0:T(8,128)(2,1)S(1)}, bf16[64,4096]{1,0:T(8,128)(2,1)}, u32[]{:S(2)}, u32[]{:S(2)}) collective-permute-start(bf16[64,4096]{1,0:T(8,128)(2,1)S(1)} %collective-permute-done.4), channel_id=1, source_target_pairs={{0,2},{2,4},{4,6},{6,8},{8,10},{10,12},{12,14},{14,0},{1,3},{3,5},... | collective-permute-start | bytes 1572872 | tf_op jit(solution)/shard_map/ppermute | solution.py:13
  88.7 135.5 %all-reduce.3.cloned.1.call-start = ((), (), s32[]{:S(2)}) async-start(), calls=%async_computation.5 | async-start | bytes 131072 | tf_op jit(solution)/shard_map/psum | solution.py:45
  97.4 57.5 %collective-permute-start.6 = (bf16[64,4096]{1,0:T(8,128)(2,1)}, bf16[64,4096]{1,0:T(8,128)(2,1)}, u32[]{:S(2)}, u32[]{:S(2)}) collective-permute-start(bf16[64,4096]{1,0:T(8,128)(2,1)} %collective-permute-done.5), channel_id=1, source_target_pairs={{0,2},{2,4},{4,6},{6,8},{8,10},{10,12},{12,14},{14,0},{1,3},{3,5},... | collective-permute-start | bytes 1572872 | tf_op jit(solution)/shard_map/ppermute | solution.py:13
  154.0 8.8 %copy-start.6 = (bf16[64,4096]{1,0:T(8,128)(2,1)S(1)}, bf16[64,4096]{1,0:T(8,128)(2,1)}, u32[]{:S(2)}) copy-start(bf16[64,4096]{1,0:T(8,128)(2,1)} %copy-done.5) | copy-start | bytes 1572868
  154.0 8.9 %copy-start.4 = (bf16[64,4096]{1,0:T(8,128)(2,1)S(1)}, bf16[64,4096]{1,0:T(8,128)(2,1)}, u32[]{:S(2)}) copy-start(bf16[64,4096]{1,0:T(8,128)(2,1)} %copy-done.3) | copy-start | bytes 1572868
  154.9 7.8 %copy-start.8 = (bf16[64,4096]{1,0:T(8,128)(2,1)S(1)}, bf16[64,4096]{1,0:T(8,128)(2,1)}, u32[]{:S(2)}) copy-start(bf16[64,4096]{1,0:T(8,128)(2,1)} %copy-done.7) | copy-start | bytes 1572868
  154.9 92.4 %reduce-scatter.4.cloned.1.call-start = ((), (), s32[]{:S(2)}) async-start(), calls=%async_computation.2 | async-start | bytes 8454144 | tf_op jit(solution)/shard_map/reduce_scatter | solution.py:18
  163.0 3.2 %copy-start.10 = (bf16[1024,4096]{1,0:T(8,128)(2,1)}, bf16[1024,4096]{1,0:T(8,128)(2,1)S(1)}, u32[]{:S(2)}) copy-start(bf16[1024,4096]{1,0:T(8,128)(2,1)S(1)} %constant_dynamic-update-slice_fusion) | copy-start | bytes 25165828
  166.3 18.0 %copy-start.12 = (u32[32]{0:T(128)S(1)}, u32[32]{0:T(128)}, u32[]{:S(2)}) copy-start(u32[32]{0:T(128)} %constant.39) | copy-start | bytes 388
  166.3 57.9 %copy-start.9 = (bf16[16,2048]{1,0:T(8,128)(2,1)S(1)}, bf16[16,2048]{1,0:T(8,128)(2,1)}, u32[]{:S(2)}) copy-start(bf16[16,2048]{1,0:T(8,128)(2,1)} %param.12) | copy-start | bytes 196612
  228.4 21.9 %copy-start.1 = (bf16[4096,64]{0,1:T(8,128)(2,1)S(1)}, bf16[4096,64]{0,1:T(8,128)(2,1)}, u32[]{:S(2)}) copy-start(bf16[4096,64]{0,1:T(8,128)(2,1)} %param.11) | copy-start | bytes 1572868
Sparse Core Ops, SparseCore 0:
  9.5 13.7 all-gather.1
  88.8 63.5 reduce-scatter.5
  155.8 68.3 all-reduce.2
  226.4 13.1 reduce-scatter.3
